TPU v7x, 32 devices: a whole 2x2x4 slice. The times are simulated.
32 devices in a mesh: grp: 2 (over x), ra: 16 (over z, y, core).
Axes of the slice: x: 2, y: 2, z: 4, core: 2. Of those that a mesh axis runs over, the one named last changes fastest.
Arguments:
- pixels: bfloat16 [1536, 168, 168], P(('grp', 'ra')), parts along dimension 0, may hold values from -6 to 6
- inverse_var: bfloat16 [1536, 128, 128], P(('grp', 'ra')), parts along dimension 0, may hold values from 0.5 to 8
- psf_taps: bfloat16 [1536, 2, 41], P(('grp', 'ra')), parts along dimension 0, may hold values from -1 to 1
- warp_table: bfloat16 [64, 128, 128], replicated, may hold values from -1 to 1
- warp_index: int32 [1536, 2], P(('grp', 'ra')), parts along dimension 0, may hold values from 0 to 63
- dest_patch: int32 [1536, 1], P(('grp', 'ra')), parts along dimension 0, may hold values from 0 to 15; in each aligned block of 48 rows (0 to 47, 48 to 95, ...) at most 3 rows name the same one
- tile_row: int32 [1536], P(('grp', 'ra')), parts along dimension 0, may hold values from 0 to 3
- tile_col: int32 [1536], P(('grp', 'ra')), parts along dimension 0, may hold values from 0 to 4
Outputs:
- coadd: float32 [1024, 8192], P('grp', 'ra'), parts along dimension 0
- weight_map: float32 [1024, 8192], P('grp', 'ra'), parts along dimension 0
There are 2 independent parts, one for each index of `grp`. A program takes and returns all parts, laid end to end along the dimension named above; an argument that names none is the same for every part. Nothing has to cross between parts.
Inputs may be any that keep to these rules, and one draw needn't show every extreme that they name: `dest_patch`: among the blocks of one device no patch is named more than 3 times; some device names some patch exactly 3 times.
All inputs are finite; a program needn't handle non-finite values.
Results may differ from a plain program's by a relative error of at most 0.0066.
Values may be sent and summed in bfloat16 or wider, within the bound.
No kernel may reach another device: no remote copies, remote signals or barrier semaphores. Data moves between devices by JAX's collectives and lax.ppermute only.
A program may use at most 128 MiB of HBM per device.

v0:
```python
import functools

import jax
import jax.numpy as jnp
from jax import lax
from jax.experimental import pallas as pl
from jax.experimental.pallas import tpu as pltpu
from jax.sharding import PartitionSpec as P


TR = 4
TC = 4
TILES = TR * (TC + 1)
IDS = 8
LATE = 2
LATE_OVER = 0
BYPASS = 1

SMEM = pl.BlockSpec(memory_space=pltpu.SMEM)
VMEM = pl.BlockSpec(memory_space=pltpu.VMEM)
ANY = pl.BlockSpec(memory_space=pl.ANY)

WHOLE = pltpu.CompilerParams(vmem_limit_bytes=67_000_000)


def dot(left, right):
    return jnp.dot(left, right, preferred_element_type=jnp.float32)


def dot_t(left, right):
    return lax.dot_general(
        left, right, (((1,), (1,)), ((), ())), preferred_element_type=jnp.float32
    )


def lanes():
    return lax.broadcasted_iota(jnp.int32, (8, 128), 1)


def staggered(row):
    return pltpu.roll(jnp.broadcast_to(row, (8, 128)), 0, 1, stride=1, stride_axis=0)


def tap_lines(taps, order, slots):
    ntaps, kinds, blocks = taps.shape
    flat = taps[...].reshape(ntaps * kinds, blocks)
    rows = -(-len(slots) // 16) * 16
    which = lax.broadcasted_iota(jnp.int32, (rows, blocks), 0)
    wanted = jnp.full((rows, blocks), -1, jnp.int32)
    for index, slot in enumerate(slots):
        wanted = jnp.where(which == index, order[slot], wanted)
    pick = wanted == lax.broadcasted_iota(jnp.int32, (rows, blocks), 1)
    mixed = dot_t(pick.astype(jnp.float32).astype(jnp.bfloat16), flat).astype(jnp.bfloat16)
    shape = (ntaps * kinds, kinds * 128)
    source = lax.broadcasted_iota(jnp.int32, shape, 0)
    lane = lax.broadcasted_iota(jnp.int32, shape, 1)
    moved = source == (lane % 128) * kinds + lane // 128
    moved &= lane % 128 < ntaps
    return dot(mixed, moved.astype(jnp.float32).astype(jnp.bfloat16))


def banded(taps, side, wide):
    base, ntaps = staggered(taps), wide - side + 1
    low, high = [], []
    for start in range(0, side, 8):
        turned = pltpu.roll(base, start, 1) if start else base
        if start + 7 + ntaps <= 128:
            low.append(turned)
            high.append(jnp.zeros_like(turned))
        else:
            low.append(jnp.where(lanes() >= 64, turned, 0.0))
            high.append(jnp.where(lanes() >= 64, 0.0, turned))
    both = jnp.concatenate([jnp.concatenate(low, 0), jnp.concatenate(high, 0)], 1)
    return both.astype(jnp.bfloat16)[:, :wide]


def slots_body(owners, capacity, count, dest, row, col, order, ids):
    me = lax.axis_index("ra")

    def clear(slot, carry):
        order[slot] = 0
        ids[slot] = TILES
        return carry

    lax.fori_loop(0, owners * capacity, clear, 0)

    def zero(owner, carry):
        count[owner] = 0
        return carry

    lax.fori_loop(0, owners, zero, 0)

    def place(block, carry):
        owner = dest[block]
        rank = count[owner]
        count[owner] = rank + 1
        slot = (owner ^ me) * capacity + rank
        order[slot] = block
        ids[slot] = row[block] * (TC + 1) + col[block]
        return carry

    lax.fori_loop(0, dest.shape[0], place, 0)


def routed(tile, route):
    if route == "all":
        return tile
    border = lax.rem(tile, TC + 1) == TC
    if route == "inner":
        return lax.select(border, TILES, tile)
    return lax.select(border, tile - TC, TILES)


def blocks_body(capacity, pieces, order, ids, widx, arrays, outs, buffers, sem, meanwhile=None):
    taps, pixels, ivar, table = arrays
    px, iv, rt, ct = buffers
    side, wide = ivar.shape[1], pixels.shape[1]
    copies = []
    steps = sorted(set(step for step, _, _ in pieces), key=[p[0] for p in pieces].index)
    for index, step in enumerate(steps):
        for rank in range(capacity):
            at = index * capacity + rank
            block = order[step * capacity + rank]
            pairs = (
                (pixels.at[block], px.at[at]),
                (ivar.at[block], iv.at[at]),
                (table.at[widx[0, block]], rt.at[at]),
                (table.at[widx[1, block]], ct.at[at]),
            )
            for kind, (source, target) in enumerate(pairs):
                copy = pltpu.make_async_copy(source, target, sem.at[kind, at])
                copy.start()
                copies.append(copy)
    if meanwhile is not None:
        meanwhile()
    slots = [step * capacity + rank for step in steps for rank in range(capacity)]
    lines = tap_lines(taps, order, slots)
    for index, step in enumerate(steps):
        at = range(index * capacity, (index + 1) * capacity)
        for copy in copies[4 * at[0] : 4 * (at[-1] + 1)]:
            copy.wait()
        cols = [banded(lines[i : i + 1, 128:], side, wide) for i in at]
        rows = [banded(lines[i : i + 1, :128], side, wide) for i in at]
        passed = [dot_t(px[i], k).astype(jnp.bfloat16) for i, k in zip(at, cols)]
        weighted = [
            (dot(k, p) * iv[i].astype(jnp.float32)).astype(jnp.bfloat16)
            for i, k, p in zip(at, rows, passed)
        ]
        middle = [
            dot(rt[i], jnp.concatenate([w, iv[i]], 1)).astype(jnp.bfloat16)
            for i, w in zip(at, weighted)
        ]
        result = []
        for i, m in zip(at, middle):
            both = jnp.concatenate([m[:, :side], m[:, side:]], 0)
            result.append(dot_t(both, ct[i]).astype(jnp.bfloat16))
        which = lax.broadcasted_iota(jnp.int32, (IDS, side), 0)
        for (owner, ranks, route), out in zip(pieces, outs):
            if owner != step:
                continue
            tiles = jnp.full((IDS, side), TILES, jnp.int32)
            for place, rank in enumerate(ranks):
                out[pl.ds(place * 2 * side, 2 * side), :] = result[rank]
                tile = routed(ids[step * capacity + rank], route)
                tiles = jnp.where(which == place, tile, tiles)
            at_end = pl.ds(len(ranks) * 2 * side, IDS)
            out[at_end, :] = tiles.astype(jnp.float32).astype(jnp.bfloat16)


def first_kernel(owners, capacity, pieces, *refs):
    dest, row, col, widx = refs[:4]
    arrays, refs = refs[4:8], refs[8:]
    order, ids = refs[:2]
    outs, refs = refs[2 : 2 + len(pieces)], refs[2 + len(pieces) :]
    step = pieces[0][0]
    first = lax.axis_index("ra") ^ step

    base = step * capacity
    for rank in range(capacity):
        refs[-2][rank] = 0
    rank = jnp.int32(0)
    for block in range(dest.shape[0]):
        refs[-2][rank] = block
        rank = rank + (dest[block] == first).astype(jnp.int32)
    for place in range(capacity):
        order[base + place] = lax.select(place < rank, refs[-2][place], 0)
    fill = functools.partial(slots_body, owners, capacity, refs[-1], dest, row, col, order, ids)
    blocks_body(capacity, pieces, order, ids, widx, arrays, outs, refs[:4], refs[4], fill)


def next_kernel(capacity, pieces, *refs):
    order, ids, widx = refs[:3]
    arrays, refs = refs[3:7], refs[8:]
    outs, refs = refs[: len(pieces)], refs[len(pieces) :]
    blocks_body(capacity, pieces, order, ids, widx, arrays, outs, refs[:4], refs[4])


def fetched(sources, targets, sem):
    copies = []
    for index, (source, target) in enumerate(zip(sources, targets)):
        copy = pltpu.make_async_copy(source, target, sem.at[index])
        copy.start()
        copies.append(copy)
    return copies


def add_parcel(parcel, side, add):
    count = parcel.shape[0] // (2 * side)
    tiles = parcel[pl.ds(count * 2 * side, IDS), :].astype(jnp.float32)
    for rank in range(count):
        tile = tiles[rank : rank + 1]
        add(jnp.max(tile).astype(jnp.int32), parcel.at[pl.ds(rank * 2 * side, 2 * side), :])


def early_kernel(count, *refs):
    parcels, (total, *buffer, sem) = refs[:count], refs[count:]
    side = total.shape[2]
    copies = fetched(parcels, buffer, sem)
    total[...] = jnp.zeros_like(total)

    def add(tile, block):
        total[tile] = total[tile] + block[...].astype(jnp.float32)

    for index, copy in enumerate(copies):
        copy.wait()
        add_parcel(buffer[index], side, add)


def border_kernel(count, total, *refs):
    parcels, (border, sums, *buffer, sem) = refs[:count], refs[count:]
    side = border.shape[2]
    columns = [total.at[row * (TC + 1) + TC] for row in range(TR)]
    targets = [sums.at[row] for row in range(TR)] + buffer
    for copy in fetched(columns + list(parcels), targets, sem):
        copy.wait()

    def add(tile, block):
        row = lax.select(lax.rem(tile, TC + 1) == TC, lax.div(tile, TC + 1), TR)
        sums[row] = sums[row] + block[...].astype(jnp.float32)

    sums[TR] = jnp.zeros_like(sums[TR])
    for index in range(count):
        add_parcel(buffer[index], side, add)
    for row in range(TR):
        border[row] = sums[row].astype(jnp.bfloat16)


def inner_kernel(count, total, *refs):
    parcels, (coadd, weight_map, edge, sums, ratio, weight, *buffer, sem, out_sem) = (
        refs[:count],
        refs[count:],
    )
    side = edge.shape[2]
    for copy in fetched([total] + list(parcels), [sums] + buffer, sem):
        copy.wait()

    def add(tile, block):
        sums[tile] = sums[tile] + block[...].astype(jnp.float32)

    for index in range(count):
        add_parcel(buffer[index], side, add)
    copies = []
    for row in range(TR):
        pairs = [(sums.at[row * (TC + 1)], edge.at[row])]
        for col in range(TC):
            both = sums[row * (TC + 1) + col]
            num, den = both[:side], both[side:]
            at = pl.ds(col * side, side)
            weight[row, :, at] = den
            ratio[row, :, at] = num / jnp.maximum(den, 1.0)
        rows = pl.ds(row * side, side)
        pairs += [(ratio.at[row], coadd.at[rows]), (weight.at[row], weight_map.at[rows])]
        for kind, (source, target) in enumerate(pairs):
            copies.append(pltpu.make_async_copy(source, target, out_sem.at[kind, row]))
            copies[-1].start()
    for copy in copies:
        copy.wait()


def edge_kernel(edge, border, coadd_in, map_in, coadd, weight_map, sums, more, num, den, sem, in_sem):
    side = edge.shape[2]
    sources = [edge.at[row] for row in range(TR)] + [border.at[row] for row in range(TR)]
    targets = [sums.at[row] for row in range(TR)] + [more.at[row] for row in range(TR)]
    arriving = fetched(sources, targets, in_sem)
    copies = []
    for row in range(TR):
        arriving[row].wait()
        arriving[TR + row].wait()
        both = sums[row] + more[row].astype(jnp.float32)
        num[row] = both[:side] / jnp.maximum(both[side:], 1.0)
        den[row] = both[side:]
        for kind, (source, target) in enumerate(((num, coadd), (den, weight_map))):
            copy = pltpu.make_async_copy(
                source.at[row],
                target.at[pl.ds(row * side, side), pl.ds(0, side)],
                sem.at[kind, row],
            )
            copy.start()
            copies.append(copy)
    for copy in copies:
        copy.wait()


def exchanged(value, owners, step, beyond=0):
    if step == 0 and not beyond:
        return value
    pairs = [(source, ((source ^ step) + beyond) % owners) for source in range(owners)]
    return lax.ppermute(value, "ra", pairs)


def passed_along(value, owners):
    return lax.ppermute(value, "ra", [(source, (source + 1) % owners) for source in range(owners)])


def planned(owners):
    half = owners // 2
    far = list(range(half, owners))
    near = list(range(half - 1, -1, -1))
    over, side = near[: half // 2], near[half // 2 : -2]
    cut = len(over) * 3 // 4
    steps = far[:3] + over[:cut] + far[3:4] + over[cut:] + far[4:5] + side + far[5:] + near[-2:]
    groups = [steps[:1], steps[1:2], steps[2:4]]
    for start in range(4, owners, 3):
        groups.append(steps[start : start + 3])
    groups[-1:] = [groups[-1][:1], groups[-1][1:]] if len(groups[-1]) > 1 else groups[-1:]
    return groups, far[-1], over[len(over) - LATE_OVER :] + far[len(far) - LATE :]


def shards(pixels, inverse_var, psf_taps, warp_table, warp_index, dest_patch, tile_row, tile_col):
    blocks, wide = pixels.shape[:2]
    side = inverse_var.shape[1]
    owners = lax.axis_size("ra")
    capacity = max(2, blocks // owners)
    bf16, f32 = jnp.bfloat16, jnp.float32
    slots = jax.ShapeDtypeStruct((owners * capacity,), jnp.int32)
    totals = (TILES + 1, 2 * side, side)

    def cost(count, flops, moved):
        return pl.CostEstimate(flops=count * flops, bytes_accessed=count * moved, transcendentals=0)

    widx = warp_index.T
    arrays = (jnp.transpose(psf_taps, (2, 1, 0)), pixels, inverse_var, warp_table)
    groups, last, slow = planned(owners)

    def buffers(count):
        return [
            pltpu.VMEM((count, wide, wide), bf16),
            pltpu.VMEM((count, side, side), bf16),
            pltpu.VMEM((count, side, side), bf16),
            pltpu.VMEM((count, side, side), bf16),
            pltpu.SemaphoreType.DMA((4, count)),
        ]

    def parcel(count):
        return jax.ShapeDtypeStruct((count * 2 * side + IDS, side), bf16)

    everything, kept = tuple(range(capacity)), capacity - min(BYPASS, capacity - 1)
    final = everything[kept:]
    cut = [(last, everything[:kept], "all"), (last, final, "inner"), (last, final, "border")]
    sent = {}
    before = None
    for index, steps in enumerate(groups):
        count = len(steps) * capacity
        pieces = []
        for step in steps:
            pieces += cut if step == last else [(step, everything, "all")]
        parcels = [parcel(len(ranks)) for _, ranks, _ in pieces]
        shared = dict(
            scratch_shapes=buffers(count),
            cost_estimate=cost(count, 30 << 20, 1 << 18),
            compiler_params=WHOLE,
            name="blocks_" + str(index),
        )
        if index == 0:
            shared["scratch_shapes"] += [
                pltpu.SMEM((capacity + 1,), jnp.int32),
                pltpu.SMEM((owners,), jnp.int32),
            ]
            order, ids, *outs = pl.pallas_call(
                functools.partial(first_kernel, owners, capacity, pieces),
                out_shape=[slots, slots] + parcels,
                in_specs=[SMEM] * 4 + [VMEM] + [ANY] * 3,
                out_specs=[SMEM] * 2 + [VMEM] * len(parcels),
                **shared,
            )(dest_patch[:, 0], tile_row, tile_col, widx, *arrays)
        else:
            outs = pl.pallas_call(
                functools.partial(next_kernel, capacity, pieces),
                out_shape=parcels,
                in_specs=[SMEM] * 3 + [VMEM] + [ANY] * 4,
                out_specs=[VMEM] * len(parcels),
                **shared,
            )(order, ids, widx, *arrays, before)
        before = outs[0]
        sent.update({(step, route): out for (step, _, route), out in zip(pieces, outs)})
    steps = [step for group in groups for step in group]
    arrived = {}
    for step in steps:
        arrived[step] = exchanged(sent[step, "all"], owners, step)
    late = [arrived[step] for step in slow]
    early = [arrived[step] for step in steps if step not in slow]
    ending = []
    for route, beyond in (("inner", 0), ("border", 1)):
        ending.append(exchanged(sent[last, route], owners, last, beyond))

    def held(parcels, others):
        scratch = [pltpu.VMEM(value.shape, bf16) for value in parcels]
        return scratch + [pltpu.SemaphoreType.DMA((len(parcels) + others,))]

    total = pl.pallas_call(
        functools.partial(early_kernel, len(early)),
        out_shape=jax.ShapeDtypeStruct(totals, f32),
        in_specs=[ANY] * len(early),
        out_specs=VMEM,
        scratch_shapes=held(early, 0),
        cost_estimate=cost(len(early) * capacity, 1 << 16, 1 << 17),
        compiler_params=WHOLE,
        name="early_sum",
    )(*early)
    border = pl.pallas_call(
        functools.partial(border_kernel, len(late)),
        out_shape=jax.ShapeDtypeStruct((TR, 2 * side, side), bf16),
        in_specs=[ANY] * (1 + len(late)),
        out_specs=VMEM,
        scratch_shapes=[pltpu.VMEM((TR + 1, 2 * side, side), f32)] + held(late, TR),
        compiler_params=WHOLE,
        name="border_sum",
    )(total, *late)
    border = passed_along(border, owners)
    rest = late + ending
    sky = jax.ShapeDtypeStruct((TR * side, TC * side), f32)
    coadd, weight_map, edge = pl.pallas_call(
        functools.partial(inner_kernel, len(rest)),
        out_shape=[sky, sky, jax.ShapeDtypeStruct((TR, 2 * side, side), f32)],
        in_specs=[ANY] * (1 + len(rest)),
        out_specs=[ANY] * 3,
        scratch_shapes=[pltpu.VMEM(totals, f32)]
        + [pltpu.VMEM((TR, side, TC * side), f32)] * 2
        + held(rest, 1)
        + [pltpu.SemaphoreType.DMA((3, TR))],
        cost_estimate=cost(1, 1 << 22, 1 << 23),
        compiler_params=WHOLE,
        name="inner",
    )(total, *rest)
    return tuple(
        pl.pallas_call(
            edge_kernel,
            out_shape=[sky, sky],
            in_specs=[ANY] * 4,
            out_specs=[ANY] * 2,
            scratch_shapes=[
                pltpu.VMEM((TR, 2 * side, side), f32),
                pltpu.VMEM((TR, 2 * side, side), bf16),
                pltpu.VMEM((TR, side, side), f32),
                pltpu.VMEM((TR, side, side), f32),
                pltpu.SemaphoreType.DMA((2, TR)),
                pltpu.SemaphoreType.DMA((2 * TR,)),
            ],
            input_output_aliases={2: 0, 3: 1},
            compiler_params=WHOLE,
            name="edge",
        )(edge, border, coadd, weight_map)
    )


def solution(mesh):
    placed = (
        P(("grp", "ra"), None, None),
        P(("grp", "ra"), None, None),
        P(("grp", "ra"), None, None),
        P(),
        P(("grp", "ra"), None),
        P(("grp", "ra"), None),
        P(("grp", "ra")),
        P(("grp", "ra")),
    )
    return jax.shard_map(
        shards,
        mesh=mesh,
        in_specs=placed,
        out_specs=(P("grp", "ra"), P("grp", "ra")),
        check_vma=False,
    )
```

profile of v0, /device:TPU:5, one launch (start us, length us, event | category | flops | bytes accessed | tf_op | source)
XLA Modules:
  0.0 105.5 jit_solution(16643926812615392676)
XLA Ops:
  0.6 3.9 %blocks_0.1 = (s32[48]{0:T(128)}, s32[48]{0:T(128)}, bf16[776,128]{1,0:T(8,128)(2,1)}) custom-call(s32[48]{0:T(128)} %bitcast.19, s32[48]{0:T(128)} %refs_1_.1, s32[48]{0:T(128)} %refs_2_.1, s32[2,48]{1,0:T(2,128)} %bitcast.11, bf16[41,2,48]{2,1,0:T(2,128)(2,1)} %bitcast.3, bf16[48,168,168]{2,1,0:T(8,128)(2,1)} %refs_4_.13, bf16[48,128,128]{2,1,0:T(8,128)(2,1)} %refs_5_.15, ...), custom_call_target="tpu_custom_call" | custom-call | flops 94371840 | bytes 786432 | tf_op jit(solution)/shard_map/blocks_0/pallas_call | solution.py:379
  4.5 2.4 %collective-permute-start = (bf16[776,128]{1,0:T(8,128)(2,1)}, bf16[776,128]{1,0:T(8,128)(2,1)}, u32[]{:S(2)}, u32[]{:S(2)}) collective-permute-start(bf16[776,128]{1,0:T(8,128)(2,1)} %get-tuple-element.24.refs_7_), channel_id=1, source_target_pairs={{0,8},{1,9},{2,10},{3,11},{4,12},{5,13},{6,14},{7,15},{8,0},{9,1},... | collective-permute-start | bytes 595976 | tf_op jit(solution)/shard_map/ppermute | solution.py:308
  6.9 3.5 %blocks_1.1.refs_7_ = bf16[776,128]{1,0:T(8,128)(2,1)} custom-call(s32[48]{0:T(128)} %get-tuple-element.25.refs_0_, s32[48]{0:T(128)} %get-tuple-element.26.refs_1_, s32[2,48]{1,0:T(2,128)} %bitcast.12, bf16[41,2,48]{2,1,0:T(2,128)(2,1)} %bitcast.4, bf16[48,168,168]{2,1,0:T(8,128)(2,1)} %refs_4_.13, bf16[48,128,128]{2,1,0:T(8,128)(2,1)} %refs_5_.15, ...), custom_call_target="tpu_custom_call" | custom-call | flops 94371840 | bytes 786432 | tf_op jit(solution)/shard_map/blocks_1/pallas_call | solution.py:387
  10.4 1.0 collective-permute-start.1
  11.3 4.5 %blocks_2.1 = (bf16[776,128]{1,0:T(8,128)(2,1)}, bf16[776,128]{1,0:T(8,128)(2,1)}) custom-call(s32[48]{0:T(128)} %get-tuple-element.25.refs_0_, s32[48]{0:T(128)} %get-tuple-element.26.refs_1_, s32[2,48]{1,0:T(2,128)} %bitcast.13, bf16[41,2,48]{2,1,0:T(2,128)(2,1)} %bitcast.5, bf16[48,168,168]{2,1,0:T(8,128)(2,1)} %refs_4_.13, ...), custom_call_target="tpu_custom_call" | custom-call | flops 188743680 | bytes 1572864 | tf_op jit(solution)/shard_map/blocks_2/pallas_call | solution.py:387
  15.8 2.3 %collective-permute-start.2 = (bf16[776,128]{1,0:T(8,128)(2,1)}, bf16[776,128]{1,0:T(8,128)(2,1)}, u32[]{:S(2)}, u32[]{:S(2)}) collective-permute-start(bf16[776,128]{1,0:T(8,128)(2,1)} %get-tuple-element.27.refs_7_), channel_id=1, source_target_pairs={{0,10},{1,11},{2,8},{3,9},{4,14},{5,15},{6,12},{7,13},{8,2},{9,3},... | collective-permute-start | bytes 595976 | tf_op jit(solution)/shard_map/ppermute | solution.py:308
  18.1 2.0 %collective-permute-start.3 = (bf16[776,128]{1,0:T(8,128)(2,1)}, bf16[776,128]{1,0:T(8,128)(2,1)}, u32[]{:S(2)}, u32[]{:S(2)}) collective-permute-start(bf16[776,128]{1,0:T(8,128)(2,1)} %get-tuple-element.28), channel_id=1, source_target_pairs={{0,7},{1,6},{2,5},{3,4},{4,3},{5,2},{6,1},{7,0},{8,15},{9,14},{10,... | collective-permute-start | bytes 595976 | tf_op jit(solution)/shard_map/ppermute | solution.py:308
  20.1 5.5 %blocks_3.1 = (bf16[776,128]{1,0:T(8,128)(2,1)}, bf16[776,128]{1,0:T(8,128)(2,1)}, bf16[776,128]{1,0:T(8,128)(2,1)}) custom-call(s32[48]{0:T(128)} %get-tuple-element.25.refs_0_, s32[48]{0:T(128)} %get-tuple-element.26.refs_1_, s32[2,48]{1,0:T(2,128)} %bitcast.14, bf16[41,2,48]{2,1,0:T(2,128)(2,1)} %bitcast.6, bf16[48,168,168]{2,1,0:T(8,128)(2,1)} %refs_4_.13, ...), custom_call_target="tpu_custom_call" | custom-call | flops 283115520 | bytes 2359296 | tf_op jit(solution)/shard_map/blocks_3/pallas_call | solution.py:387
  25.6 0.3 collective-permute-start.4
  25.9 5.5 %blocks_4.1 = (bf16[776,128]{1,0:T(8,128)(2,1)}, bf16[776,128]{1,0:T(8,128)(2,1)}, bf16[776,128]{1,0:T(8,128)(2,1)}) custom-call(s32[48]{0:T(128)} %get-tuple-element.25.refs_0_, s32[48]{0:T(128)} %get-tuple-element.26.refs_1_, s32[2,48]{1,0:T(2,128)} %bitcast.15, bf16[41,2,48]{2,1,0:T(2,128)(2,1)} %bitcast.7, bf16[48,168,168]{2,1,0:T(8,128)(2,1)} %refs_4_.13, ...), custom_call_target="tpu_custom_call" | custom-call | flops 283115520 | bytes 2359296 | tf_op jit(solution)/shard_map/blocks_4/pallas_call | solution.py:387
  31.4 0.0 collective-permute-done.refs_0_
  31.4 2.0 %collective-permute-start.5 = (bf16[776,128]{1,0:T(8,128)(2,1)}, bf16[776,128]{1,0:T(8,128)(2,1)}, u32[]{:S(2)}, u32[]{:S(2)}) collective-permute-start(bf16[776,128]{1,0:T(8,128)(2,1)} %get-tuple-element.30), channel_id=1, source_target_pairs={{0,5},{1,4},{2,7},{3,6},{4,1},{5,0},{6,3},{7,2},{8,13},{9,12},{10,... | collective-permute-start | bytes 595976 | tf_op jit(solution)/shard_map/ppermute | solution.py:308
  33.5 0.0 collective-permute-done.1.refs_1_
  33.5 1.0 collective-permute-start.6
  34.4 0.0 collective-permute-done.2.refs_2_
  34.5 0.2 collective-permute-start.7
  34.6 0.0 collective-permute-done.3.refs_3_
  34.6 2.8 %collective-permute-start.8 = (bf16[776,128]{1,0:T(8,128)(2,1)}, bf16[776,128]{1,0:T(8,128)(2,1)}, u32[]{:S(2)}, u32[]{:S(2)}) collective-permute-start(bf16[776,128]{1,0:T(8,128)(2,1)} %get-tuple-element.33), channel_id=1, source_target_pairs={{0,12},{1,13},{2,14},{3,15},{4,8},{5,9},{6,10},{7,11},{8,4},{9,5},... | collective-permute-start | bytes 595976 | tf_op jit(solution)/shard_map/ppermute | solution.py:308
  37.4 3.4 %collective-permute-done.4.refs_4_ = bf16[776,128]{1,0:T(8,128)(2,1)} collective-permute-done((bf16[776,128]{1,0:T(8,128)(2,1)}, bf16[776,128]{1,0:T(8,128)(2,1)}, u32[]{:S(2)}, u32[]{:S(2)}) %collective-permute-start.4) | collective-permute-done | bytes 198688 | tf_op jit(solution)/shard_map/ppermute | solution.py:308
  40.8 2.3 %collective-permute-start.9 = (bf16[776,128]{1,0:T(8,128)(2,1)}, bf16[776,128]{1,0:T(8,128)(2,1)}, u32[]{:S(2)}, u32[]{:S(2)}) collective-permute-start(bf16[776,128]{1,0:T(8,128)(2,1)} %get-tuple-element.34), channel_id=1, source_target_pairs={{0,3},{1,2},{2,1},{3,0},{4,7},{5,6},{6,5},{7,4},{8,11},{9,10},{10,... | collective-permute-start | bytes 595976 | tf_op jit(solution)/shard_map/ppermute | solution.py:308
  43.1 5.5 %blocks_5.1 = (bf16[776,128]{1,0:T(8,128)(2,1)}, bf16[776,128]{1,0:T(8,128)(2,1)}, bf16[776,128]{1,0:T(8,128)(2,1)}) custom-call(s32[48]{0:T(128)} %get-tuple-element.25.refs_0_, s32[48]{0:T(128)} %get-tuple-element.26.refs_1_, s32[2,48]{1,0:T(2,128)} %bitcast.16, bf16[41,2,48]{2,1,0:T(2,128)(2,1)} %bitcast.8, bf16[48,168,168]{2,1,0:T(8,128)(2,1)} %refs_4_.13, ...), custom_call_target="tpu_custom_call" | custom-call | flops 283115520 | bytes 2359296 | tf_op jit(solution)/shard_map/blocks_5/pallas_call | solution.py:387
  48.6 3.5 %blocks_6.1 = (bf16[520,128]{1,0:T(8,128)(2,1)}, bf16[264,128]{1,0:T(8,128)(2,1)}, bf16[264,128]{1,0:T(8,128)(2,1)}) custom-call(s32[48]{0:T(128)} %get-tuple-element.25.refs_0_, s32[48]{0:T(128)} %get-tuple-element.26.refs_1_, s32[2,48]{1,0:T(2,128)} %bitcast.17, bf16[41,2,48]{2,1,0:T(2,128)(2,1)} %bitcast.9, bf16[48,168,168]{2,1,0:T(8,128)(2,1)} %refs_4_.13, ...), custom_call_target="tpu_custom_call" | custom-call | flops 94371840 | bytes 786432 | tf_op jit(solution)/shard_map/blocks_6/pallas_call | solution.py:387
  52.1 4.5 %blocks_7.1 = (bf16[776,128]{1,0:T(8,128)(2,1)}, bf16[776,128]{1,0:T(8,128)(2,1)}) custom-call(s32[48]{0:T(128)} %get-tuple-element.25.refs_0_, s32[48]{0:T(128)} %get-tuple-element.26.refs_1_, s32[2,48]{1,0:T(2,128)} %bitcast.18, bf16[41,2,48]{2,1,0:T(2,128)(2,1)} %bitcast.10, bf16[48,168,168]{2,1,0:T(8,128)(2,1)} %refs_4_.13, ...), custom_call_target="tpu_custom_call" | custom-call | flops 188743680 | bytes 1572864 | tf_op jit(solution)/shard_map/blocks_7/pallas_call | solution.py:387
  56.6 0.0 collective-permute-done.5.refs_5_
  56.6 0.1 collective-permute-start.10
  56.7 0.0 collective-permute-done.6.refs_6_
  56.7 4.6 %collective-permute-start.11 = (bf16[776,128]{1,0:T(8,128)(2,1)}, bf16[776,128]{1,0:T(8,128)(2,1)}, u32[]{:S(2)}, u32[]{:S(2)}) collective-permute-start(bf16[776,128]{1,0:T(8,128)(2,1)} %get-tuple-element.36), channel_id=1, source_target_pairs={{0,13},{1,12},{2,15},{3,14},{4,9},{5,8},{6,11},{7,10},{8,5},{9,4},... | collective-permute-start | bytes 595976 | tf_op jit(solution)/shard_map/ppermute | solution.py:308
  61.3 0.0 collective-permute-done.7.refs_7_
  61.3 0.2 collective-permute-start.12
  61.5 0.0 collective-permute-done.8.refs_8_
  61.5 0.9 collective-permute-start.13
  62.4 0.0 collective-permute-done.9.refs_9_
  62.4 3.8 %collective-permute-start.14 = (bf16[520,128]{1,0:T(8,128)(2,1)}, bf16[520,128]{1,0:T(8,128)(2,1)}, u32[]{:S(2)}, u32[]{:S(2)}) collective-permute-start(bf16[520,128]{1,0:T(8,128)(2,1)} %get-tuple-element.37.refs_7_), channel_id=1, source_target_pairs={{0,15},{1,14},{2,13},{3,12},{4,11},{5,10},{6,9},{7,8},{8,7},{9,6},... | collective-permute-start | bytes 399368 | tf_op jit(solution)/shard_map/ppermute | solution.py:308
  66.2 0.0 collective-permute-done.10.refs_10_
  66.2 0.6 collective-permute-done.11.refs_11_
  66.8 0.0 collective-permute-done.12.refs_12_
  66.8 4.8 %early_sum.1.total = f32[21,256,128]{2,1,0:T(8,128)} custom-call(bf16[776,128]{1,0:T(8,128)(2,1)} %collective-permute-done.refs_0_, bf16[776,128]{1,0:T(8,128)(2,1)} %collective-permute-done.1.refs_1_, bf16[776,128]{1,0:T(8,128)(2,1)} %collective-permute-done.2.refs_2_, bf16[776,128]{1,0:T(8,128)(2,1)} %collective-permute-done.3.refs_3_, ...), custom_call_target="tpu_custom_call" | custom-call | flops 2752512 | bytes 5505024 | tf_op jit(solution)/shard_map/early_sum/pallas_call | solution.py:410
  71.5 3.6 %collective-permute-done.14.refs_1_ = bf16[520,128]{1,0:T(8,128)(2,1)} collective-permute-done((bf16[520,128]{1,0:T(8,128)(2,1)}, bf16[520,128]{1,0:T(8,128)(2,1)}, u32[]{:S(2)}, u32[]{:S(2)}) %collective-permute-start.14) | collective-permute-done | bytes 133152 | tf_op jit(solution)/shard_map/ppermute | solution.py:308
  75.1 0.0 collective-permute-done.13.refs_0_
  75.1 2.2 %border_sum.1 = bf16[4,256,128]{2,1,0:T(8,128)(2,1)} custom-call(f32[21,256,128]{2,1,0:T(8,128)} %early_sum.1.total, bf16[776,128]{1,0:T(8,128)(2,1)} %collective-permute-done.13.refs_0_, bf16[520,128]{1,0:T(8,128)(2,1)} %collective-permute-done.14.refs_1_), custom_call_target="tpu_custom_call" | custom-call | tf_op jit(solution)/shard_map/border_sum/pallas_call | solution.py:420
  77.3 14.3 %collective-permute-start.17 = (bf16[4,256,128]{2,1,0:T(8,128)(2,1)}, bf16[4,256,128]{2,1,0:T(8,128)(2,1)}, u32[]{:S(2)}, u32[]{:S(2)}) collective-permute-start(bf16[4,256,128]{2,1,0:T(8,128)(2,1)} %border_sum.1), channel_id=1, source_target_pairs={{0,1},{1,2},{2,3},{3,4},{4,5},{5,6},{6,7},{7,8},{8,9},{9,10},{10,1... | collective-permute-start | bytes 786440 | tf_op jit(solution)/shard_map/ppermute | solution.py:312
  91.6 0.0 collective-permute-start.15
  91.6 1.9 %collective-permute-start.16 = (bf16[264,128]{1,0:T(8,128)(2,1)}, bf16[264,128]{1,0:T(8,128)(2,1)}, u32[]{:S(2)}, u32[]{:S(2)}) collective-permute-start(bf16[264,128]{1,0:T(8,128)(2,1)} %get-tuple-element.42), channel_id=1, source_target_pairs={{0,0},{1,15},{2,14},{3,13},{4,12},{5,11},{6,10},{7,9},{8,8},{9,7},... | collective-permute-start | bytes 202760 | tf_op jit(solution)/shard_map/ppermute | solution.py:308
  93.6 4.8 %collective-permute-done.15.refs_2_ = bf16[264,128]{1,0:T(8,128)(2,1)} collective-permute-done((bf16[264,128]{1,0:T(8,128)(2,1)}, bf16[264,128]{1,0:T(8,128)(2,1)}, u32[]{:S(2)}, u32[]{:S(2)}) %collective-permute-start.15) | collective-permute-done | bytes 67616 | tf_op jit(solution)/shard_map/ppermute | solution.py:308
  98.4 1.4 %collective-permute-done.16.refs_3_ = bf16[264,128]{1,0:T(8,128)(2,1)} collective-permute-done((bf16[264,128]{1,0:T(8,128)(2,1)}, bf16[264,128]{1,0:T(8,128)(2,1)}, u32[]{:S(2)}, u32[]{:S(2)}) %collective-permute-start.16) | collective-permute-done | bytes 67616 | tf_op jit(solution)/shard_map/ppermute | solution.py:308
  99.8 3.7 %inner.1 = (f32[512,512]{1,0:T(8,128)}, f32[512,512]{1,0:T(8,128)}, f32[4,256,128]{2,1,0:T(8,128)}) custom-call(f32[21,256,128]{2,1,0:T(8,128)} %early_sum.1.total, bf16[776,128]{1,0:T(8,128)(2,1)} %collective-permute-done.13.refs_0_, bf16[520,128]{1,0:T(8,128)(2,1)} %collective-permute-done.14.refs_1_, bf16[264,128]{1,0:T(8,128)(2,1)} %collective-permute-done.15.refs_2_, ...), custom_call_target="tpu_custom_call" | custom-call | flops 4194304 | bytes 8388608 | tf_op jit(solution)/shard_map/inner/pallas_call | solution.py:432
  103.5 0.0 collective-permute-done.17.border
  103.5 2.0 %edge.1 = (f32[512,512]{1,0:T(8,128)}, f32[512,512]{1,0:T(8,128)}) custom-call(f32[4,256,128]{2,1,0:T(8,128)} %get-tuple-element.43.edge, bf16[4,256,128]{2,1,0:T(8,128)(2,1)} %collective-permute-done.17.border, f32[512,512]{1,0:T(8,128)} %get-tuple-element.44.coadd_in, ...), custom_call_target="tpu_custom_call", output_to_operand_aliasing={{0}: (2, {}), {1}: (3, {})} | custom-call | tf_op jit(solution)/shard_map/edge/pallas_call | solution.py:446
Async XLA Ops:
  4.5 26.9 %collective-permute-start = (bf16[776,128]{1,0:T(8,128)(2,1)}, bf16[776,128]{1,0:T(8,128)(2,1)}, u32[]{:S(2)}, u32[]{:S(2)}) collective-permute-start(bf16[776,128]{1,0:T(8,128)(2,1)} %get-tuple-element.24.refs_7_), channel_id=1, source_target_pairs={{0,8},{1,9},{2,10},{3,11},{4,12},{5,13},{6,14},{7,15},{8,0},{9,1},... | collective-permute-start | bytes 595976 | tf_op jit(solution)/shard_map/ppermute | solution.py:308
  10.4 23.1 %collective-permute-start.1 = (bf16[776,128]{1,0:T(8,128)(2,1)}, bf16[776,128]{1,0:T(8,128)(2,1)}, u32[]{:S(2)}, u32[]{:S(2)}) collective-permute-start(bf16[776,128]{1,0:T(8,128)(2,1)} %blocks_1.1.refs_7_), channel_id=1, source_target_pairs={{0,9},{1,8},{2,11},{3,10},{4,13},{5,12},{6,15},{7,14},{8,1},{9,0},... | collective-permute-start | bytes 595976 | tf_op jit(solution)/shard_map/ppermute | solution.py:308
  15.8 18.6 %collective-permute-start.2 = (bf16[776,128]{1,0:T(8,128)(2,1)}, bf16[776,128]{1,0:T(8,128)(2,1)}, u32[]{:S(2)}, u32[]{:S(2)}) collective-permute-start(bf16[776,128]{1,0:T(8,128)(2,1)} %get-tuple-element.27.refs_7_), channel_id=1, source_target_pairs={{0,10},{1,11},{2,8},{3,9},{4,14},{5,15},{6,12},{7,13},{8,2},{9,3},... | collective-permute-start | bytes 595976 | tf_op jit(solution)/shard_map/ppermute | solution.py:308
  18.1 16.5 %collective-permute-start.3 = (bf16[776,128]{1,0:T(8,128)(2,1)}, bf16[776,128]{1,0:T(8,128)(2,1)}, u32[]{:S(2)}, u32[]{:S(2)}) collective-permute-start(bf16[776,128]{1,0:T(8,128)(2,1)} %get-tuple-element.28), channel_id=1, source_target_pairs={{0,7},{1,6},{2,5},{3,4},{4,3},{5,2},{6,1},{7,0},{8,15},{9,14},{10,... | collective-permute-start | bytes 595976 | tf_op jit(solution)/shard_map/ppermute | solution.py:308
  25.6 15.2 %collective-permute-start.4 = (bf16[776,128]{1,0:T(8,128)(2,1)}, bf16[776,128]{1,0:T(8,128)(2,1)}, u32[]{:S(2)}, u32[]{:S(2)}) collective-permute-start(bf16[776,128]{1,0:T(8,128)(2,1)} %get-tuple-element.29.refs_7_), channel_id=1, source_target_pairs={{0,6},{1,7},{2,4},{3,5},{4,2},{5,3},{6,0},{7,1},{8,14},{9,15},{10,... | collective-permute-start | bytes 595976 | tf_op jit(solution)/shard_map/ppermute | solution.py:308
  31.4 25.2 %collective-permute-start.5 = (bf16[776,128]{1,0:T(8,128)(2,1)}, bf16[776,128]{1,0:T(8,128)(2,1)}, u32[]{:S(2)}, u32[]{:S(2)}) collective-permute-start(bf16[776,128]{1,0:T(8,128)(2,1)} %get-tuple-element.30), channel_id=1, source_target_pairs={{0,5},{1,4},{2,7},{3,6},{4,1},{5,0},{6,3},{7,2},{8,13},{9,12},{10,... | collective-permute-start | bytes 595976 | tf_op jit(solution)/shard_map/ppermute | solution.py:308
  33.5 23.2 %collective-permute-start.6 = (bf16[776,128]{1,0:T(8,128)(2,1)}, bf16[776,128]{1,0:T(8,128)(2,1)}, u32[]{:S(2)}, u32[]{:S(2)}) collective-permute-start(bf16[776,128]{1,0:T(8,128)(2,1)} %get-tuple-element.31), channel_id=1, source_target_pairs={{0,11},{1,10},{2,9},{3,8},{4,15},{5,14},{6,13},{7,12},{8,3},{9,2},... | collective-permute-start | bytes 595976 | tf_op jit(solution)/shard_map/ppermute | solution.py:308
  34.5 26.9 %collective-permute-start.7 = (bf16[776,128]{1,0:T(8,128)(2,1)}, bf16[776,128]{1,0:T(8,128)(2,1)}, u32[]{:S(2)}, u32[]{:S(2)}) collective-permute-start(bf16[776,128]{1,0:T(8,128)(2,1)} %get-tuple-element.32.refs_7_), channel_id=1, source_target_pairs={{0,4},{1,5},{2,6},{3,7},{4,0},{5,1},{6,2},{7,3},{8,12},{9,13},{10,... | collective-permute-start | bytes 595976 | tf_op jit(solution)/shard_map/ppermute | solution.py:308
  34.6 26.9 %collective-permute-start.8 = (bf16[776,128]{1,0:T(8,128)(2,1)}, bf16[776,128]{1,0:T(8,128)(2,1)}, u32[]{:S(2)}, u32[]{:S(2)}) collective-permute-start(bf16[776,128]{1,0:T(8,128)(2,1)} %get-tuple-element.33), channel_id=1, source_target_pairs={{0,12},{1,13},{2,14},{3,15},{4,8},{5,9},{6,10},{7,11},{8,4},{9,5},... | collective-permute-start | bytes 595976 | tf_op jit(solution)/shard_map/ppermute | solution.py:308
  40.8 21.6 %collective-permute-start.9 = (bf16[776,128]{1,0:T(8,128)(2,1)}, bf16[776,128]{1,0:T(8,128)(2,1)}, u32[]{:S(2)}, u32[]{:S(2)}) collective-permute-start(bf16[776,128]{1,0:T(8,128)(2,1)} %get-tuple-element.34), channel_id=1, source_target_pairs={{0,3},{1,2},{2,1},{3,0},{4,7},{5,6},{6,5},{7,4},{8,11},{9,10},{10,... | collective-permute-start | bytes 595976 | tf_op jit(solution)/shard_map/ppermute | solution.py:308
  56.6 9.6 %collective-permute-start.10 = (bf16[776,128]{1,0:T(8,128)(2,1)}, bf16[776,128]{1,0:T(8,128)(2,1)}, u32[]{:S(2)}, u32[]{:S(2)}) collective-permute-start(bf16[776,128]{1,0:T(8,128)(2,1)} %get-tuple-element.35.refs_7_), channel_id=1, source_target_pairs={{0,2},{1,3},{2,0},{3,1},{4,6},{5,7},{6,4},{7,5},{8,10},{9,11},{10,... | collective-permute-start | bytes 595976 | tf_op jit(solution)/shard_map/ppermute | solution.py:308
  56.7 10.0 %collective-permute-start.11 = (bf16[776,128]{1,0:T(8,128)(2,1)}, bf16[776,128]{1,0:T(8,128)(2,1)}, u32[]{:S(2)}, u32[]{:S(2)}) collective-permute-start(bf16[776,128]{1,0:T(8,128)(2,1)} %get-tuple-element.36), channel_id=1, source_target_pairs={{0,13},{1,12},{2,15},{3,14},{4,9},{5,8},{6,11},{7,10},{8,5},{9,4},... | collective-permute-start | bytes 595976 | tf_op jit(solution)/shard_map/ppermute | solution.py:308
  61.3 5.4 %collective-permute-start.12 = (bf16[776,128]{1,0:T(8,128)(2,1)}, bf16[776,128]{1,0:T(8,128)(2,1)}, u32[]{:S(2)}, u32[]{:S(2)}) collective-permute-start(bf16[776,128]{1,0:T(8,128)(2,1)} %get-tuple-element.38), channel_id=1, source_target_pairs={{0,1},{1,0},{2,3},{3,2},{4,5},{5,4},{6,7},{7,6},{8,9},{9,8},{10,11... | collective-permute-start | bytes 595976 | tf_op jit(solution)/shard_map/ppermute | solution.py:308
  61.5 13.6 %collective-permute-start.13 = (bf16[776,128]{1,0:T(8,128)(2,1)}, bf16[776,128]{1,0:T(8,128)(2,1)}, u32[]{:S(2)}, u32[]{:S(2)}) collective-permute-start(bf16[776,128]{1,0:T(8,128)(2,1)} %get-tuple-element.40), channel_id=1, source_target_pairs={{0,14},{1,15},{2,12},{3,13},{4,10},{5,11},{6,8},{7,9},{8,6},{9,7},... | collective-permute-start | bytes 595976 | tf_op jit(solution)/shard_map/ppermute | solution.py:308
  62.4 12.7 %collective-permute-start.14 = (bf16[520,128]{1,0:T(8,128)(2,1)}, bf16[520,128]{1,0:T(8,128)(2,1)}, u32[]{:S(2)}, u32[]{:S(2)}) collective-permute-start(bf16[520,128]{1,0:T(8,128)(2,1)} %get-tuple-element.37.refs_7_), channel_id=1, source_target_pairs={{0,15},{1,14},{2,13},{3,12},{4,11},{5,10},{6,9},{7,8},{8,7},{9,6},... | collective-permute-start | bytes 399368 | tf_op jit(solution)/shard_map/ppermute | solution.py:308
  77.3 26.2 %collective-permute-start.17 = (bf16[4,256,128]{2,1,0:T(8,128)(2,1)}, bf16[4,256,128]{2,1,0:T(8,128)(2,1)}, u32[]{:S(2)}, u32[]{:S(2)}) collective-permute-start(bf16[4,256,128]{2,1,0:T(8,128)(2,1)} %border_sum.1), channel_id=1, source_target_pairs={{0,1},{1,2},{2,3},{3,4},{4,5},{5,6},{6,7},{7,8},{8,9},{9,10},{10,1... | collective-permute-start | bytes 786440 | tf_op jit(solution)/shard_map/ppermute | solution.py:312
  91.6 6.7 %collective-permute-start.15 = (bf16[264,128]{1,0:T(8,128)(2,1)}, bf16[264,128]{1,0:T(8,128)(2,1)}, u32[]{:S(2)}, u32[]{:S(2)}) collective-permute-start(bf16[264,128]{1,0:T(8,128)(2,1)} %get-tuple-element.41), channel_id=1, source_target_pairs={{0,15},{1,14},{2,13},{3,12},{4,11},{5,10},{6,9},{7,8},{8,7},{9,6},... | collective-permute-start | bytes 202760 | tf_op jit(solution)/shard_map/ppermute | solution.py:308
  91.6 8.2 %collective-permute-start.16 = (bf16[264,128]{1,0:T(8,128)(2,1)}, bf16[264,128]{1,0:T(8,128)(2,1)}, u32[]{:S(2)}, u32[]{:S(2)}) collective-permute-start(bf16[264,128]{1,0:T(8,128)(2,1)} %get-tuple-element.42), channel_id=1, source_target_pairs={{0,0},{1,15},{2,14},{3,13},{4,12},{5,11},{6,10},{7,9},{8,8},{9,7},... | collective-permute-start | bytes 202760 | tf_op jit(solution)/shard_map/ppermute | solution.py:308
where the time goes:
time: 107 us; the launch traced here: 106 us
  Pallas kernels  48.9 us (46%)
  starting transfers between devices  42 us (39%)
  waiting for transfers between devices  13.8 us (13%)
    pallas_call x7, Pallas kernels, shards(): pl.pallas_call(functools.partial(next_kernel, capacity, pieces), out_shap...  32.4 us
    ppermute x17, starting transfers between devices, exchanged(): return lax.ppermute(value, 'ra', pairs)  27.7 us
    ppermute x1, starting transfers between devices, passed_along(): lax.ppermute(value, 'ra', [(source, (source + 1) % owners) for source in...  14.3 us
    ppermute x17, waiting for transfers between devices, exchanged(): return lax.ppermute(value, 'ra', pairs)  13.8 us
    pallas_call x1, Pallas kernels, shards(): pl.pallas_call(functools.partial(early_kernel, len(early)), out_shape=jax...  4.77 us
    pallas_call x1, Pallas kernels, shards(): pl.pallas_call(functools.partial(first_kernel, owners, capacity, pieces),...  3.88 us
    pallas_call x1, Pallas kernels, shards(): pl.pallas_call(functools.partial(inner_kernel, len(rest)), out_shape=[sky...  3.67 us
    pallas_call x1, Pallas kernels, shards(): pl.pallas_call(functools.partial(border_kernel, len(late)), out_shape=jax...  2.18 us
  transfers between devices with their start and end apart: 18, of which 5 were waited for; matrix products, arithmetic and copies ran while one was open for 0% of the time, Pallas kernels for 39%

commit v1 on v0

--- a/solution.py
+++ b/solution.py
@@ -231,14 +231,15 @@
     side = border.shape[2]
     columns = [total.at[row * (TC + 1) + TC] for row in range(TR)]
     targets = [sums.at[row] for row in range(TR)] + buffer
-    for copy in fetched(columns + list(parcels), targets, sem):
+    copies = fetched(columns + list(parcels), targets, sem)
+    sums[TR] = jnp.zeros_like(sums[TR])
+    for copy in copies:
         copy.wait()
 
     def add(tile, block):
         row = lax.select(lax.rem(tile, TC + 1) == TC, lax.div(tile, TC + 1), TR)
         sums[row] = sums[row] + block[...].astype(jnp.float32)
 
-    sums[TR] = jnp.zeros_like(sums[TR])
     for index in range(count):
         add_parcel(buffer[index], side, add)
     for row in range(TR):
@@ -320,9 +321,8 @@
     cut = len(over) * 3 // 4
     steps = far[:3] + over[:cut] + far[3:4] + over[cut:] + far[4:5] + side + far[5:] + near[-2:]
     groups = [steps[:1], steps[1:2], steps[2:4]]
-    for start in range(4, owners, 3):
-        groups.append(steps[start : start + 3])
-    groups[-1:] = [groups[-1][:1], groups[-1][1:]] if len(groups[-1]) > 1 else groups[-1:]
+    for start in range(4, owners, 4):
+        groups.append(steps[start : start + 4])
     return groups, far[-1], over[len(over) - LATE_OVER :] + far[len(far) - LATE :]
 
 

time: 107 us -> 102 us (0.953)
  Pallas kernels: 48.9 us -> 43.9 us
    pallas_call x7 -> x5, Pallas kernels: 32.4 us -> 27.4 us  [shards(): pl.pallas_call(functools.partial(next_kernel, capacity, pieces), out_shap...]
    ppermute x17, starting transfers between devices: 27.7 us -> 26.1 us  [exchanged(): return lax.ppermute(value, 'ra', pairs)]
    ppermute x1, starting transfers between devices: 14.3 us -> 15.7 us  [passed_along(): lax.ppermute(value, 'ra', [(source, (source + 1) % owners) for source in...]
  transfers between devices with their start and end apart: 18 -> 18, of which waited for: 5 -> 8; matrix products, arithmetic and copies ran while one was open for 0% -> 0% of each run, Pallas kernels for 39% -> 35%
where the time goes in v1:
time: 102 us; the launch traced here: 101 us
  Pallas kernels  43.9 us (43%)
  starting transfers between devices  41.7 us (41%)
  waiting for transfers between devices  14.6 us (14%)
    pallas_call x5, Pallas kernels, shards(): pl.pallas_call(functools.partial(next_kernel, capacity, pieces), out_shap...  27.4 us
    ppermute x17, starting transfers between devices, exchanged(): return lax.ppermute(value, 'ra', pairs)  26.1 us
    ppermute x1, starting transfers between devices, passed_along(): lax.ppermute(value, 'ra', [(source, (source + 1) % owners) for source in...  15.7 us
    ppermute x17, waiting for transfers between devices, exchanged(): return lax.ppermute(value, 'ra', pairs)  14.6 us
    pallas_call x1, Pallas kernels, shards(): pl.pallas_call(functools.partial(early_kernel, len(early)), out_shape=jax...  4.78 us
    pallas_call x1, Pallas kernels, shards(): pl.pallas_call(functools.partial(first_kernel, owners, capacity, pieces),...  3.88 us
    pallas_call x1, Pallas kernels, shards(): pl.pallas_call(functools.partial(inner_kernel, len(rest)), out_shape=[sky...  3.67 us
    pallas_call x1, Pallas kernels, shards(): pl.pallas_call(functools.partial(border_kernel, len(late)), out_shape=jax...  2.19 us
  transfers between devices with their start and end apart: 18, of which 8 were waited for; matrix products, arithmetic and copies ran while one was open for 0% of the time, Pallas kernels for 35%

profile of v1, /device:TPU:5, one launch (start us, length us, event | category | flops | bytes accessed | tf_op | source)
XLA Modules:
  0.0 101.0 jit_solution(14344300421689161686)
XLA Ops:
  0.6 3.9 %blocks_0.1 = (s32[48]{0:T(128)}, s32[48]{0:T(128)}, bf16[776,128]{1,0:T(8,128)(2,1)}) custom-call(s32[48]{0:T(128)} %bitcast.15, s32[48]{0:T(128)} %refs_1_.1, s32[48]{0:T(128)} %refs_2_.1, s32[2,48]{1,0:T(2,128)} %bitcast.9, bf16[41,2,48]{2,1,0:T(2,128)(2,1)} %bitcast.3, bf16[48,168,168]{2,1,0:T(8,128)(2,1)} %refs_4_.9, bf16[48,128,128]{2,1,0:T(8,128)(2,1)} %refs_5_.11, ...), custom_call_target="tpu_custom_call" | custom-call | flops 94371840 | bytes 786432 | tf_op jit(solution)/shard_map/blocks_0/pallas_call | solution.py:379
  4.5 2.4 %collective-permute-start = (bf16[776,128]{1,0:T(8,128)(2,1)}, bf16[776,128]{1,0:T(8,128)(2,1)}, u32[]{:S(2)}, u32[]{:S(2)}) collective-permute-start(bf16[776,128]{1,0:T(8,128)(2,1)} %get-tuple-element.24.refs_7_), channel_id=1, source_target_pairs={{0,8},{1,9},{2,10},{3,11},{4,12},{5,13},{6,14},{7,15},{8,0},{9,1},... | collective-permute-start | bytes 595976 | tf_op jit(solution)/shard_map/ppermute | solution.py:309
  6.9 3.5 %blocks_1.1.refs_7_ = bf16[776,128]{1,0:T(8,128)(2,1)} custom-call(s32[48]{0:T(128)} %get-tuple-element.25.refs_0_, s32[48]{0:T(128)} %get-tuple-element.26.refs_1_, s32[2,48]{1,0:T(2,128)} %bitcast.10, bf16[41,2,48]{2,1,0:T(2,128)(2,1)} %bitcast.4, bf16[48,168,168]{2,1,0:T(8,128)(2,1)} %refs_4_.9, bf16[48,128,128]{2,1,0:T(8,128)(2,1)} %refs_5_.11, ...), custom_call_target="tpu_custom_call" | custom-call | flops 94371840 | bytes 786432 | tf_op jit(solution)/shard_map/blocks_1/pallas_call | solution.py:387
  10.4 1.0 collective-permute-start.1
  11.3 4.5 %blocks_2.1 = (bf16[776,128]{1,0:T(8,128)(2,1)}, bf16[776,128]{1,0:T(8,128)(2,1)}) custom-call(s32[48]{0:T(128)} %get-tuple-element.25.refs_0_, s32[48]{0:T(128)} %get-tuple-element.26.refs_1_, s32[2,48]{1,0:T(2,128)} %bitcast.11, bf16[41,2,48]{2,1,0:T(2,128)(2,1)} %bitcast.5, bf16[48,168,168]{2,1,0:T(8,128)(2,1)} %refs_4_.9, ...), custom_call_target="tpu_custom_call" | custom-call | flops 188743680 | bytes 1572864 | tf_op jit(solution)/shard_map/blocks_2/pallas_call | solution.py:387
  15.8 2.3 %collective-permute-start.2 = (bf16[776,128]{1,0:T(8,128)(2,1)}, bf16[776,128]{1,0:T(8,128)(2,1)}, u32[]{:S(2)}, u32[]{:S(2)}) collective-permute-start(bf16[776,128]{1,0:T(8,128)(2,1)} %get-tuple-element.27.refs_7_), channel_id=1, source_target_pairs={{0,10},{1,11},{2,8},{3,9},{4,14},{5,15},{6,12},{7,13},{8,2},{9,3},... | collective-permute-start | bytes 595976 | tf_op jit(solution)/shard_map/ppermute | solution.py:309
  18.2 2.0 %collective-permute-start.3 = (bf16[776,128]{1,0:T(8,128)(2,1)}, bf16[776,128]{1,0:T(8,128)(2,1)}, u32[]{:S(2)}, u32[]{:S(2)}) collective-permute-start(bf16[776,128]{1,0:T(8,128)(2,1)} %get-tuple-element.28), channel_id=1, source_target_pairs={{0,7},{1,6},{2,5},{3,4},{4,3},{5,2},{6,1},{7,0},{8,15},{9,14},{10,... | collective-permute-start | bytes 595976 | tf_op jit(solution)/shard_map/ppermute | solution.py:309
  20.1 6.5 %blocks_3.1 = (bf16[776,128]{1,0:T(8,128)(2,1)}, bf16[776,128]{1,0:T(8,128)(2,1)}, bf16[776,128]{1,0:T(8,128)(2,1)}, bf16[776,128]{1,0:T(8,128)(2,1)}) custom-call(s32[48]{0:T(128)} %get-tuple-element.25.refs_0_, s32[48]{0:T(128)} %get-tuple-element.26.refs_1_, s32[2,48]{1,0:T(2,128)} %bitcast.12, bf16[41,2,48]{2,1,0:T(2,128)(2,1)} %bitcast.6, ...), custom_call_target="tpu_custom_call" | custom-call | flops 377487360 | bytes 3145728 | tf_op jit(solution)/shard_map/blocks_3/pallas_call | solution.py:387
  26.6 0.4 collective-permute-start.4
  27.0 0.0 collective-permute-done.refs_0_
  27.0 2.0 %collective-permute-start.5 = (bf16[776,128]{1,0:T(8,128)(2,1)}, bf16[776,128]{1,0:T(8,128)(2,1)}, u32[]{:S(2)}, u32[]{:S(2)}) collective-permute-start(bf16[776,128]{1,0:T(8,128)(2,1)} %get-tuple-element.30), channel_id=1, source_target_pairs={{0,5},{1,4},{2,7},{3,6},{4,1},{5,0},{6,3},{7,2},{8,13},{9,12},{10,... | collective-permute-start | bytes 595976 | tf_op jit(solution)/shard_map/ppermute | solution.py:309
  28.9 2.0 %collective-permute-done.1.refs_1_ = bf16[776,128]{1,0:T(8,128)(2,1)} collective-permute-done((bf16[776,128]{1,0:T(8,128)(2,1)}, bf16[776,128]{1,0:T(8,128)(2,1)}, u32[]{:S(2)}, u32[]{:S(2)}) %collective-permute-start.1) | collective-permute-done | bytes 198688 | tf_op jit(solution)/shard_map/ppermute | solution.py:309
  30.9 0.0 collective-permute-start.6
  30.9 2.2 %collective-permute-done.2.refs_2_ = bf16[776,128]{1,0:T(8,128)(2,1)} collective-permute-done((bf16[776,128]{1,0:T(8,128)(2,1)}, bf16[776,128]{1,0:T(8,128)(2,1)}, u32[]{:S(2)}, u32[]{:S(2)}) %collective-permute-start.2) | collective-permute-done | bytes 198688 | tf_op jit(solution)/shard_map/ppermute | solution.py:309
  33.1 1.2 %collective-permute-start.7 = (bf16[776,128]{1,0:T(8,128)(2,1)}, bf16[776,128]{1,0:T(8,128)(2,1)}, u32[]{:S(2)}, u32[]{:S(2)}) collective-permute-start(bf16[776,128]{1,0:T(8,128)(2,1)} %get-tuple-element.32), channel_id=1, source_target_pairs={{0,4},{1,5},{2,6},{3,7},{4,0},{5,1},{6,2},{7,3},{8,12},{9,13},{10,... | collective-permute-start | bytes 595976 | tf_op jit(solution)/shard_map/ppermute | solution.py:309
  34.4 6.5 %blocks_4.1 = (bf16[776,128]{1,0:T(8,128)(2,1)}, bf16[776,128]{1,0:T(8,128)(2,1)}, bf16[776,128]{1,0:T(8,128)(2,1)}, bf16[776,128]{1,0:T(8,128)(2,1)}) custom-call(s32[48]{0:T(128)} %get-tuple-element.25.refs_0_, s32[48]{0:T(128)} %get-tuple-element.26.refs_1_, s32[2,48]{1,0:T(2,128)} %bitcast.13, bf16[41,2,48]{2,1,0:T(2,128)(2,1)} %bitcast.7, ...), custom_call_target="tpu_custom_call" | custom-call | flops 377487360 | bytes 3145728 | tf_op jit(solution)/shard_map/blocks_4/pallas_call | solution.py:387
  40.9 0.0 collective-permute-done.3.refs_3_
  40.9 2.8 %collective-permute-start.8 = (bf16[776,128]{1,0:T(8,128)(2,1)}, bf16[776,128]{1,0:T(8,128)(2,1)}, u32[]{:S(2)}, u32[]{:S(2)}) collective-permute-start(bf16[776,128]{1,0:T(8,128)(2,1)} %get-tuple-element.33.refs_7_), channel_id=1, source_target_pairs={{0,12},{1,13},{2,14},{3,15},{4,8},{5,9},{6,10},{7,11},{8,4},{9,5},... | collective-permute-start | bytes 595976 | tf_op jit(solution)/shard_map/ppermute | solution.py:309
  43.7 0.0 collective-permute-done.4.refs_4_
  43.7 2.1 %collective-permute-start.9 = (bf16[776,128]{1,0:T(8,128)(2,1)}, bf16[776,128]{1,0:T(8,128)(2,1)}, u32[]{:S(2)}, u32[]{:S(2)}) collective-permute-start(bf16[776,128]{1,0:T(8,128)(2,1)} %get-tuple-element.34), channel_id=1, source_target_pairs={{0,3},{1,2},{2,1},{3,0},{4,7},{5,6},{6,5},{7,4},{8,11},{9,10},{10,... | collective-permute-start | bytes 595976 | tf_op jit(solution)/shard_map/ppermute | solution.py:309
  45.8 6.5 %blocks_5.1 = (bf16[776,128]{1,0:T(8,128)(2,1)}, bf16[520,128]{1,0:T(8,128)(2,1)}, bf16[264,128]{1,0:T(8,128)(2,1)}, bf16[264,128]{1,0:T(8,128)(2,1)}, bf16[776,...) custom-call(s32[48]{0:T(128)} %get-tuple-element.25.refs_0_, s32[48]{0:T(128)} %get-tuple-element.26.refs_1_, s32[2,48]{1,0:T(2,128)} %bitcast.14, ...), custom_call_target="tpu_custom_call" | custom-call | flops 377487360 | bytes 3145728 | tf_op jit(solution)/shard_map/blocks_5/pallas_call | solution.py:387
  52.3 0.3 collective-permute-done.5.refs_5_
  52.6 0.0 collective-permute-start.10
  52.6 0.0 collective-permute-done.6.refs_6_
  52.6 2.4 %collective-permute-start.11 = (bf16[776,128]{1,0:T(8,128)(2,1)}, bf16[776,128]{1,0:T(8,128)(2,1)}, u32[]{:S(2)}, u32[]{:S(2)}) collective-permute-start(bf16[776,128]{1,0:T(8,128)(2,1)} %get-tuple-element.36), channel_id=1, source_target_pairs={{0,13},{1,12},{2,15},{3,14},{4,9},{5,8},{6,11},{7,10},{8,5},{9,4},... | collective-permute-start | bytes 595976 | tf_op jit(solution)/shard_map/ppermute | solution.py:309
  55.0 0.5 collective-permute-done.7.refs_7_
  55.5 1.2 %collective-permute-start.12 = (bf16[776,128]{1,0:T(8,128)(2,1)}, bf16[776,128]{1,0:T(8,128)(2,1)}, u32[]{:S(2)}, u32[]{:S(2)}) collective-permute-start(bf16[776,128]{1,0:T(8,128)(2,1)} %get-tuple-element.37), channel_id=1, source_target_pairs={{0,1},{1,0},{2,3},{3,2},{4,5},{5,4},{6,7},{7,6},{8,9},{9,8},{10,11... | collective-permute-start | bytes 595976 | tf_op jit(solution)/shard_map/ppermute | solution.py:309
  56.7 0.0 collective-permute-done.8.refs_8_
  56.7 2.2 %collective-permute-start.13 = (bf16[776,128]{1,0:T(8,128)(2,1)}, bf16[776,128]{1,0:T(8,128)(2,1)}, u32[]{:S(2)}, u32[]{:S(2)}) collective-permute-start(bf16[776,128]{1,0:T(8,128)(2,1)} %get-tuple-element.39), channel_id=1, source_target_pairs={{0,14},{1,15},{2,12},{3,13},{4,10},{5,11},{6,8},{7,9},{8,6},{9,7},... | collective-permute-start | bytes 595976 | tf_op jit(solution)/shard_map/ppermute | solution.py:309
  58.9 0.0 collective-permute-done.9.refs_9_
  58.9 2.2 %collective-permute-start.14 = (bf16[520,128]{1,0:T(8,128)(2,1)}, bf16[520,128]{1,0:T(8,128)(2,1)}, u32[]{:S(2)}, u32[]{:S(2)}) collective-permute-start(bf16[520,128]{1,0:T(8,128)(2,1)} %get-tuple-element.40), channel_id=1, source_target_pairs={{0,15},{1,14},{2,13},{3,12},{4,11},{5,10},{6,9},{7,8},{8,7},{9,6},... | collective-permute-start | bytes 399368 | tf_op jit(solution)/shard_map/ppermute | solution.py:309
  61.1 0.0 collective-permute-done.10.refs_10_
  61.1 1.0 collective-permute-done.11.refs_11_
  62.1 0.0 collective-permute-done.12.refs_12_
  62.1 4.8 %early_sum.1.total = f32[21,256,128]{2,1,0:T(8,128)} custom-call(bf16[776,128]{1,0:T(8,128)(2,1)} %collective-permute-done.refs_0_, bf16[776,128]{1,0:T(8,128)(2,1)} %collective-permute-done.1.refs_1_, bf16[776,128]{1,0:T(8,128)(2,1)} %collective-permute-done.2.refs_2_, bf16[776,128]{1,0:T(8,128)(2,1)} %collective-permute-done.3.refs_3_, ...), custom_call_target="tpu_custom_call" | custom-call | flops 2752512 | bytes 5505024 | tf_op jit(solution)/shard_map/early_sum/pallas_call | solution.py:410
  66.9 2.4 %collective-permute-done.14.refs_1_ = bf16[520,128]{1,0:T(8,128)(2,1)} collective-permute-done((bf16[520,128]{1,0:T(8,128)(2,1)}, bf16[520,128]{1,0:T(8,128)(2,1)}, u32[]{:S(2)}, u32[]{:S(2)}) %collective-permute-start.14) | collective-permute-done | bytes 133152 | tf_op jit(solution)/shard_map/ppermute | solution.py:309
  69.3 0.0 collective-permute-done.13.refs_0_
  69.3 2.2 %border_sum.1 = bf16[4,256,128]{2,1,0:T(8,128)(2,1)} custom-call(f32[21,256,128]{2,1,0:T(8,128)} %early_sum.1.total, bf16[776,128]{1,0:T(8,128)(2,1)} %collective-permute-done.13.refs_0_, bf16[520,128]{1,0:T(8,128)(2,1)} %collective-permute-done.14.refs_1_), custom_call_target="tpu_custom_call" | custom-call | tf_op jit(solution)/shard_map/border_sum/pallas_call | solution.py:420
  71.5 15.7 %collective-permute-start.17 = (bf16[4,256,128]{2,1,0:T(8,128)(2,1)}, bf16[4,256,128]{2,1,0:T(8,128)(2,1)}, u32[]{:S(2)}, u32[]{:S(2)}) collective-permute-start(bf16[4,256,128]{2,1,0:T(8,128)(2,1)} %border_sum.1), channel_id=1, source_target_pairs={{0,1},{1,2},{2,3},{3,4},{4,5},{5,6},{6,7},{7,8},{8,9},{9,10},{10,1... | collective-permute-start | bytes 786440 | tf_op jit(solution)/shard_map/ppermute | solution.py:313
  87.1 0.0 collective-permute-start.15
  87.2 1.9 %collective-permute-start.16 = (bf16[264,128]{1,0:T(8,128)(2,1)}, bf16[264,128]{1,0:T(8,128)(2,1)}, u32[]{:S(2)}, u32[]{:S(2)}) collective-permute-start(bf16[264,128]{1,0:T(8,128)(2,1)} %get-tuple-element.42), channel_id=1, source_target_pairs={{0,0},{1,15},{2,14},{3,13},{4,12},{5,11},{6,10},{7,9},{8,8},{9,7},... | collective-permute-start | bytes 202760 | tf_op jit(solution)/shard_map/ppermute | solution.py:309
  89.1 4.8 %collective-permute-done.15.refs_2_ = bf16[264,128]{1,0:T(8,128)(2,1)} collective-permute-done((bf16[264,128]{1,0:T(8,128)(2,1)}, bf16[264,128]{1,0:T(8,128)(2,1)}, u32[]{:S(2)}, u32[]{:S(2)}) %collective-permute-start.15) | collective-permute-done | bytes 67616 | tf_op jit(solution)/shard_map/ppermute | solution.py:309
  93.9 1.4 %collective-permute-done.16.refs_3_ = bf16[264,128]{1,0:T(8,128)(2,1)} collective-permute-done((bf16[264,128]{1,0:T(8,128)(2,1)}, bf16[264,128]{1,0:T(8,128)(2,1)}, u32[]{:S(2)}, u32[]{:S(2)}) %collective-permute-start.16) | collective-permute-done | bytes 67616 | tf_op jit(solution)/shard_map/ppermute | solution.py:309
  95.3 3.7 %inner.1 = (f32[512,512]{1,0:T(8,128)}, f32[512,512]{1,0:T(8,128)}, f32[4,256,128]{2,1,0:T(8,128)}) custom-call(f32[21,256,128]{2,1,0:T(8,128)} %early_sum.1.total, bf16[776,128]{1,0:T(8,128)(2,1)} %collective-permute-done.13.refs_0_, bf16[520,128]{1,0:T(8,128)(2,1)} %collective-permute-done.14.refs_1_, bf16[264,128]{1,0:T(8,128)(2,1)} %collective-permute-done.15.refs_2_, ...), custom_call_target="tpu_custom_call" | custom-call | flops 4194304 | bytes 8388608 | tf_op jit(solution)/shard_map/inner/pallas_call | solution.py:432
  99.0 0.0 collective-permute-done.17.border
  99.0 2.0 %edge.1 = (f32[512,512]{1,0:T(8,128)}, f32[512,512]{1,0:T(8,128)}) custom-call(f32[4,256,128]{2,1,0:T(8,128)} %get-tuple-element.43.edge, bf16[4,256,128]{2,1,0:T(8,128)(2,1)} %collective-permute-done.17.border, f32[512,512]{1,0:T(8,128)} %get-tuple-element.44.coadd_in, ...), custom_call_target="tpu_custom_call", output_to_operand_aliasing={{0}: (2, {}), {1}: (3, {})} | custom-call | tf_op jit(solution)/shard_map/edge/pallas_call | solution.py:446
Async XLA Ops:
  4.5 22.5 %collective-permute-start = (bf16[776,128]{1,0:T(8,128)(2,1)}, bf16[776,128]{1,0:T(8,128)(2,1)}, u32[]{:S(2)}, u32[]{:S(2)}) collective-permute-start(bf16[776,128]{1,0:T(8,128)(2,1)} %get-tuple-element.24.refs_7_), channel_id=1, source_target_pairs={{0,8},{1,9},{2,10},{3,11},{4,12},{5,13},{6,14},{7,15},{8,0},{9,1},... | collective-permute-start | bytes 595976 | tf_op jit(solution)/shard_map/ppermute | solution.py:309
  10.4 20.6 %collective-permute-start.1 = (bf16[776,128]{1,0:T(8,128)(2,1)}, bf16[776,128]{1,0:T(8,128)(2,1)}, u32[]{:S(2)}, u32[]{:S(2)}) collective-permute-start(bf16[776,128]{1,0:T(8,128)(2,1)} %blocks_1.1.refs_7_), channel_id=1, source_target_pairs={{0,9},{1,8},{2,11},{3,10},{4,13},{5,12},{6,15},{7,14},{8,1},{9,0},... | collective-permute-start | bytes 595976 | tf_op jit(solution)/shard_map/ppermute | solution.py:309
  15.8 17.3 %collective-permute-start.2 = (bf16[776,128]{1,0:T(8,128)(2,1)}, bf16[776,128]{1,0:T(8,128)(2,1)}, u32[]{:S(2)}, u32[]{:S(2)}) collective-permute-start(bf16[776,128]{1,0:T(8,128)(2,1)} %get-tuple-element.27.refs_7_), channel_id=1, source_target_pairs={{0,10},{1,11},{2,8},{3,9},{4,14},{5,15},{6,12},{7,13},{8,2},{9,3},... | collective-permute-start | bytes 595976 | tf_op jit(solution)/shard_map/ppermute | solution.py:309
  18.2 22.7 %collective-permute-start.3 = (bf16[776,128]{1,0:T(8,128)(2,1)}, bf16[776,128]{1,0:T(8,128)(2,1)}, u32[]{:S(2)}, u32[]{:S(2)}) collective-permute-start(bf16[776,128]{1,0:T(8,128)(2,1)} %get-tuple-element.28), channel_id=1, source_target_pairs={{0,7},{1,6},{2,5},{3,4},{4,3},{5,2},{6,1},{7,0},{8,15},{9,14},{10,... | collective-permute-start | bytes 595976 | tf_op jit(solution)/shard_map/ppermute | solution.py:309
  26.6 17.1 %collective-permute-start.4 = (bf16[776,128]{1,0:T(8,128)(2,1)}, bf16[776,128]{1,0:T(8,128)(2,1)}, u32[]{:S(2)}, u32[]{:S(2)}) collective-permute-start(bf16[776,128]{1,0:T(8,128)(2,1)} %get-tuple-element.29.refs_7_), channel_id=1, source_target_pairs={{0,6},{1,7},{2,4},{3,5},{4,2},{5,3},{6,0},{7,1},{8,14},{9,15},{10,... | collective-permute-start | bytes 595976 | tf_op jit(solution)/shard_map/ppermute | solution.py:309
  27.0 25.6 %collective-permute-start.5 = (bf16[776,128]{1,0:T(8,128)(2,1)}, bf16[776,128]{1,0:T(8,128)(2,1)}, u32[]{:S(2)}, u32[]{:S(2)}) collective-permute-start(bf16[776,128]{1,0:T(8,128)(2,1)} %get-tuple-element.30), channel_id=1, source_target_pairs={{0,5},{1,4},{2,7},{3,6},{4,1},{5,0},{6,3},{7,2},{8,13},{9,12},{10,... | collective-permute-start | bytes 595976 | tf_op jit(solution)/shard_map/ppermute | solution.py:309
  30.9 21.7 %collective-permute-start.6 = (bf16[776,128]{1,0:T(8,128)(2,1)}, bf16[776,128]{1,0:T(8,128)(2,1)}, u32[]{:S(2)}, u32[]{:S(2)}) collective-permute-start(bf16[776,128]{1,0:T(8,128)(2,1)} %get-tuple-element.31), channel_id=1, source_target_pairs={{0,11},{1,10},{2,9},{3,8},{4,15},{5,14},{6,13},{7,12},{8,3},{9,2},... | collective-permute-start | bytes 595976 | tf_op jit(solution)/shard_map/ppermute | solution.py:309
  33.1 22.4 %collective-permute-start.7 = (bf16[776,128]{1,0:T(8,128)(2,1)}, bf16[776,128]{1,0:T(8,128)(2,1)}, u32[]{:S(2)}, u32[]{:S(2)}) collective-permute-start(bf16[776,128]{1,0:T(8,128)(2,1)} %get-tuple-element.32), channel_id=1, source_target_pairs={{0,4},{1,5},{2,6},{3,7},{4,0},{5,1},{6,2},{7,3},{8,12},{9,13},{10,... | collective-permute-start | bytes 595976 | tf_op jit(solution)/shard_map/ppermute | solution.py:309
  40.9 15.9 %collective-permute-start.8 = (bf16[776,128]{1,0:T(8,128)(2,1)}, bf16[776,128]{1,0:T(8,128)(2,1)}, u32[]{:S(2)}, u32[]{:S(2)}) collective-permute-start(bf16[776,128]{1,0:T(8,128)(2,1)} %get-tuple-element.33.refs_7_), channel_id=1, source_target_pairs={{0,12},{1,13},{2,14},{3,15},{4,8},{5,9},{6,10},{7,11},{8,4},{9,5},... | collective-permute-start | bytes 595976 | tf_op jit(solution)/shard_map/ppermute | solution.py:309
  43.7 15.2 %collective-permute-start.9 = (bf16[776,128]{1,0:T(8,128)(2,1)}, bf16[776,128]{1,0:T(8,128)(2,1)}, u32[]{:S(2)}, u32[]{:S(2)}) collective-permute-start(bf16[776,128]{1,0:T(8,128)(2,1)} %get-tuple-element.34), channel_id=1, source_target_pairs={{0,3},{1,2},{2,1},{3,0},{4,7},{5,6},{6,5},{7,4},{8,11},{9,10},{10,... | collective-permute-start | bytes 595976 | tf_op jit(solution)/shard_map/ppermute | solution.py:309
  52.6 8.5 %collective-permute-start.10 = (bf16[776,128]{1,0:T(8,128)(2,1)}, bf16[776,128]{1,0:T(8,128)(2,1)}, u32[]{:S(2)}, u32[]{:S(2)}) collective-permute-start(bf16[776,128]{1,0:T(8,128)(2,1)} %get-tuple-element.35), channel_id=1, source_target_pairs={{0,2},{1,3},{2,0},{3,1},{4,6},{5,7},{6,4},{7,5},{8,10},{9,11},{10,... | collective-permute-start | bytes 595976 | tf_op jit(solution)/shard_map/ppermute | solution.py:309
  52.6 9.5 %collective-permute-start.11 = (bf16[776,128]{1,0:T(8,128)(2,1)}, bf16[776,128]{1,0:T(8,128)(2,1)}, u32[]{:S(2)}, u32[]{:S(2)}) collective-permute-start(bf16[776,128]{1,0:T(8,128)(2,1)} %get-tuple-element.36), channel_id=1, source_target_pairs={{0,13},{1,12},{2,15},{3,14},{4,9},{5,8},{6,11},{7,10},{8,5},{9,4},... | collective-permute-start | bytes 595976 | tf_op jit(solution)/shard_map/ppermute | solution.py:309
  55.5 6.6 %collective-permute-start.12 = (bf16[776,128]{1,0:T(8,128)(2,1)}, bf16[776,128]{1,0:T(8,128)(2,1)}, u32[]{:S(2)}, u32[]{:S(2)}) collective-permute-start(bf16[776,128]{1,0:T(8,128)(2,1)} %get-tuple-element.37), channel_id=1, source_target_pairs={{0,1},{1,0},{2,3},{3,2},{4,5},{5,4},{6,7},{7,6},{8,9},{9,8},{10,11... | collective-permute-start | bytes 595976 | tf_op jit(solution)/shard_map/ppermute | solution.py:309
  56.7 12.6 %collective-permute-start.13 = (bf16[776,128]{1,0:T(8,128)(2,1)}, bf16[776,128]{1,0:T(8,128)(2,1)}, u32[]{:S(2)}, u32[]{:S(2)}) collective-permute-start(bf16[776,128]{1,0:T(8,128)(2,1)} %get-tuple-element.39), channel_id=1, source_target_pairs={{0,14},{1,15},{2,12},{3,13},{4,10},{5,11},{6,8},{7,9},{8,6},{9,7},... | collective-permute-start | bytes 595976 | tf_op jit(solution)/shard_map/ppermute | solution.py:309
  58.9 10.4 %collective-permute-start.14 = (bf16[520,128]{1,0:T(8,128)(2,1)}, bf16[520,128]{1,0:T(8,128)(2,1)}, u32[]{:S(2)}, u32[]{:S(2)}) collective-permute-start(bf16[520,128]{1,0:T(8,128)(2,1)} %get-tuple-element.40), channel_id=1, source_target_pairs={{0,15},{1,14},{2,13},{3,12},{4,11},{5,10},{6,9},{7,8},{8,7},{9,6},... | collective-permute-start | bytes 399368 | tf_op jit(solution)/shard_map/ppermute | solution.py:309
  71.5 27.5 %collective-permute-start.17 = (bf16[4,256,128]{2,1,0:T(8,128)(2,1)}, bf16[4,256,128]{2,1,0:T(8,128)(2,1)}, u32[]{:S(2)}, u32[]{:S(2)}) collective-permute-start(bf16[4,256,128]{2,1,0:T(8,128)(2,1)} %border_sum.1), channel_id=1, source_target_pairs={{0,1},{1,2},{2,3},{3,4},{4,5},{5,6},{6,7},{7,8},{8,9},{9,10},{10,1... | collective-permute-start | bytes 786440 | tf_op jit(solution)/shard_map/ppermute | solution.py:313
  87.1 6.7 %collective-permute-start.15 = (bf16[264,128]{1,0:T(8,128)(2,1)}, bf16[264,128]{1,0:T(8,128)(2,1)}, u32[]{:S(2)}, u32[]{:S(2)}) collective-permute-start(bf16[264,128]{1,0:T(8,128)(2,1)} %get-tuple-element.41), channel_id=1, source_target_pairs={{0,15},{1,14},{2,13},{3,12},{4,11},{5,10},{6,9},{7,8},{8,7},{9,6},... | collective-permute-start | bytes 202760 | tf_op jit(solution)/shard_map/ppermute | solution.py:309
  87.2 8.2 %collective-permute-start.16 = (bf16[264,128]{1,0:T(8,128)(2,1)}, bf16[264,128]{1,0:T(8,128)(2,1)}, u32[]{:S(2)}, u32[]{:S(2)}) collective-permute-start(bf16[264,128]{1,0:T(8,128)(2,1)} %get-tuple-element.42), channel_id=1, source_target_pairs={{0,0},{1,15},{2,14},{3,13},{4,12},{5,11},{6,10},{7,9},{8,8},{9,7},... | collective-permute-start | bytes 202760 | tf_op jit(solution)/shard_map/ppermute | solution.py:309
